TPU v7x, 32 devices: a whole 2x2x4 slice. The times are simulated.
32 devices in a mesh: bond: 8 (over y, x, core), outer: 4 (over z).
Axes of the slice: x: 2, y: 2, z: 4, core: 2. Of those that a mesh axis runs over, the one named last changes fastest.
Arguments:
- upper: bfloat16 [128, 128, 128], P(None, 'bond'), may hold values from -4 to 4
- lower: bfloat16 [128, 128, 8, 128], P(None, 'bond', 'outer'), may hold values from -4 to 4
- isometry: bfloat16 [16384, 128], P(('bond', 'outer')), may hold values from -0.046875 to 0.046875
Outputs:
- coarse: float32 [128, 8, 128], P('bond', 'outer')
All inputs are finite; a program needn't handle non-finite values.
Results may differ from a plain program's by a relative error of at most 0.004.
Values may be sent and summed in bfloat16 or wider, within the bound.
A program may use at most 64 MiB of HBM per device.

v0:
```python
import jax
import jax.numpy as jnp
from jax import lax
from jax.sharding import PartitionSpec as P


def on_device(upper, lower, isometry):
    grouped = lax.all_gather(isometry, "outer", axis=0, tiled=True)
    gathered = lax.all_gather(grouped, "bond", axis=0, tiled=True)
    upper_local, lower_local = (
        lax.all_to_all(upper, "bond", split_axis=0, concat_axis=1, tiled=True),
        lax.all_to_all(lower, "bond", split_axis=0, concat_axis=1, tiled=True),
    )
    width = gathered.shape[1]
    iso_full = gathered.reshape(width, width, width)
    members = upper_local.shape[0]
    lower_count = lower_local.shape[2]
    own_rows = width // lax.axis_size("bond")

    def member(index, total):
        upper_slab = lax.dynamic_index_in_dim(upper_local, index, 0, keepdims=False)
        lower_slab = lax.dynamic_index_in_dim(lower_local, index, 0, keepdims=False)
        joined = jnp.einsum(
            "lr,lkx->rkx", upper_slab, iso_full, preferred_element_type=jnp.float32
        ).astype(jnp.bfloat16)
        paired = jnp.einsum(
            "rkx,kds->drxs", joined, lower_slab, preferred_element_type=jnp.float32
        ).astype(jnp.bfloat16)
        return total + jnp.einsum(
            "drxs,rsy->xdy", paired, iso_full, preferred_element_type=jnp.float32
        )

    start_total = jnp.zeros((lax.axis_size("bond") * own_rows, lower_count, width), jnp.float32)
    return lax.psum_scatter(
        lax.fori_loop(0, members, member, start_total), "bond", scatter_dimension=0, tiled=True
    )


def solution(mesh):
    return jax.shard_map(
        on_device,
        mesh=mesh,
        in_specs=(
            P(None, "bond", None),
            P(None, "bond", "outer", None),
            P(("bond", "outer"), None),
        ),
        out_specs=P("bond", "outer", None),
        check_vma=False,
    )
```

profile of v0, /device:TPU:0, one launch (start us, length us, event | category | flops | bytes accessed | tf_op | source)
XLA Modules:
  0.0 397.6 jit_solution(4449285008628463018)
XLA Ops:
  6.5 19.3 %all_gather.6 = bf16[2048,128]{1,0:T(8,128)(2,1)} all-gather(bf16[512,128]{1,0:T(8,128)(2,1)} %param.7), channel_id=1, replica_groups=mesh['bond'=8,'outer'=4] {'outer'}, dimensions={0}, use_global_device_ids=true | all-gather | bytes 655360 | tf_op jit(solution)/shard_map/all_gather | solution.py:8
  25.9 16.5 %all_to_all.36 = bf16[128,16,128]{2,1,0:T(8,128)(2,1)S(1)} all-to-all(bf16[128,16,128]{2,1,0:T(8,128)(2,1)} %param.5), channel_id=1, replica_groups=mesh['bond'=8,'outer'=4] {'bond'}, dimensions={0} | all-to-all | bytes 1048576 | tf_op jit(solution)/shard_map/all_to_all | solution.py:11
  46.0 25.5 %all-to-all-done = bf16[128,16,2,128]{3,2,1,0:T(2,128)(2,1)S(1)} async-done(((bf16[128,16,2,128]{3,2,1,0:T(2,128)(2,1)}), bf16[128,16,2,128]{3,2,1,0:T(2,128)(2,1)S(1)}, u32[]{:S(2)}, u32[]{:S(2)}) %all-to-all-start) | async-done | bytes 1048608 | tf_op jit(solution)/shard_map/all_to_all | solution.py:12
  73.2 264.3 %while.14 = (s32[]{:T(128)}, f32[128,2,128]{2,0,1:T(8,128)S(1)}, bf16[16,128,2,128]{3,2,1,0:T(2,128)(2,1)S(1)}, bf16[16,128,128]{2,1,0:T(8,128)(2,1)S(1)}, bf16[...) while((s32[]{:T(128)}, f32[128,2,128]{2,0,1:T(8,128)S(1)}, ...), condition=%wide.region_1.2_spmd.clone, body=%wide.region_0.1_spmd.clone.sunk | while | flops 2688614400 | bytes 17268832 | solution.py:35
  73.2 7.6 %fusion.44 = bf16[128,128,128]{2,0,1:T(8,128)(2,1)} fusion(bf16[128,128,128]{2,1,0:T(8,128)(2,1)} %get-tuple-element.177, bf16[16,128,128]{2,1,0:T(8,128)(2,1)S(1)} %get-tuple-element.176, s32[]{:T(128)} %get-tuple-element.166), kind=kOutput, calls=%fused_computation.7.clone.1 | convolution fusion | flops 536870912 | bytes 8421380 | tf_op jit(solution)/shard_map/while/body/eval_jaxpr/lr,lkx->rkx/dot_general | solution.py:23
  80.8 8.9 %fusion.45 = f32[128,2,128]{2,0,1:T(8,128)S(1)} fusion(bf16[128,128,128]{2,1,0:T(8,128)(2,1)} %get-tuple-element.177, bf16[128,128,128]{2,0,1:T(8,128)(2,1)} %fusion.44, f32[128,2,128]{2,0,1:T(8,128)S(1)} %get-tuple-element.167, bf16[128,2,128,1]{2,1,0,3:T(2,128)(2,1)S(1)} %dynamic-slice_bitcast_fusion.2, pred[]{:T(512)S(6)} %compare.3), kind=kOutput, calls=%fused_computation.10.clone.1 | convolution fusion | flops 2151743488 | bytes 8716289 | tf_op jit(solution)/shard_map/while/body/eval_jaxpr/drxs,rsy->xdy/dot_general | solution.py:29
  97.3 8.9 %fusion.45 = f32[128,2,128]{2,0,1:T(8,128)S(1)} fusion(bf16[128,128,128]{2,1,0:T(8,128)(2,1)} %get-tuple-element.177, bf16[128,128,128]{2,0,1:T(8,128)(2,1)} %fusion.44, f32[128,2,128]{2,0,1:T(8,128)S(1)} %get-tuple-element.167, bf16[128,2,128,1]{2,1,0,3:T(2,128)(2,1)S(1)} %dynamic-slice_bitcast_fusion.2, pred[]{:T(512)S(6)} %compare.3), kind=kOutput, calls=%fused_computation.10.clone.1 | convolution fusion | flops 2151743488 | bytes 8716289 | tf_op jit(solution)/shard_map/while/body/eval_jaxpr/drxs,rsy->xdy/dot_general | solution.py:29
  106.2 7.6 %fusion.44 = bf16[128,128,128]{2,0,1:T(8,128)(2,1)} fusion(bf16[128,128,128]{2,1,0:T(8,128)(2,1)} %get-tuple-element.177, bf16[16,128,128]{2,1,0:T(8,128)(2,1)S(1)} %get-tuple-element.176, s32[]{:T(128)} %get-tuple-element.166), kind=kOutput, calls=%fused_computation.7.clone.1 | convolution fusion | flops 536870912 | bytes 8421380 | tf_op jit(solution)/shard_map/while/body/eval_jaxpr/lr,lkx->rkx/dot_general | solution.py:23
  113.8 8.9 %fusion.45 = f32[128,2,128]{2,0,1:T(8,128)S(1)} fusion(bf16[128,128,128]{2,1,0:T(8,128)(2,1)} %get-tuple-element.177, bf16[128,128,128]{2,0,1:T(8,128)(2,1)} %fusion.44, f32[128,2,128]{2,0,1:T(8,128)S(1)} %get-tuple-element.167, bf16[128,2,128,1]{2,1,0,3:T(2,128)(2,1)S(1)} %dynamic-slice_bitcast_fusion.2, pred[]{:T(512)S(6)} %compare.3), kind=kOutput, calls=%fused_computation.10.clone.1 | convolution fusion | flops 2151743488 | bytes 8716289 | tf_op jit(solution)/shard_map/while/body/eval_jaxpr/drxs,rsy->xdy/dot_general | solution.py:29
  122.8 7.6 %fusion.44 = bf16[128,128,128]{2,0,1:T(8,128)(2,1)} fusion(bf16[128,128,128]{2,1,0:T(8,128)(2,1)} %get-tuple-element.177, bf16[16,128,128]{2,1,0:T(8,128)(2,1)S(1)} %get-tuple-element.176, s32[]{:T(128)} %get-tuple-element.166), kind=kOutput, calls=%fused_computation.7.clone.1 | convolution fusion | flops 536870912 | bytes 8421380 | tf_op jit(solution)/shard_map/while/body/eval_jaxpr/lr,lkx->rkx/dot_general | solution.py:23
  130.4 8.9 %fusion.45 = f32[128,2,128]{2,0,1:T(8,128)S(1)} fusion(bf16[128,128,128]{2,1,0:T(8,128)(2,1)} %get-tuple-element.177, bf16[128,128,128]{2,0,1:T(8,128)(2,1)} %fusion.44, f32[128,2,128]{2,0,1:T(8,128)S(1)} %get-tuple-element.167, bf16[128,2,128,1]{2,1,0,3:T(2,128)(2,1)S(1)} %dynamic-slice_bitcast_fusion.2, pred[]{:T(512)S(6)} %compare.3), kind=kOutput, calls=%fused_computation.10.clone.1 | convolution fusion | flops 2151743488 | bytes 8716289 | tf_op jit(solution)/shard_map/while/body/eval_jaxpr/drxs,rsy->xdy/dot_general | solution.py:29
  146.9 8.9 %fusion.45 = f32[128,2,128]{2,0,1:T(8,128)S(1)} fusion(bf16[128,128,128]{2,1,0:T(8,128)(2,1)} %get-tuple-element.177, bf16[128,128,128]{2,0,1:T(8,128)(2,1)} %fusion.44, f32[128,2,128]{2,0,1:T(8,128)S(1)} %get-tuple-element.167, bf16[128,2,128,1]{2,1,0,3:T(2,128)(2,1)S(1)} %dynamic-slice_bitcast_fusion.2, pred[]{:T(512)S(6)} %compare.3), kind=kOutput, calls=%fused_computation.10.clone.1 | convolution fusion | flops 2151743488 | bytes 8716289 | tf_op jit(solution)/shard_map/while/body/eval_jaxpr/drxs,rsy->xdy/dot_general | solution.py:29
  163.4 8.9 %fusion.45 = f32[128,2,128]{2,0,1:T(8,128)S(1)} fusion(bf16[128,128,128]{2,1,0:T(8,128)(2,1)} %get-tuple-element.177, bf16[128,128,128]{2,0,1:T(8,128)(2,1)} %fusion.44, f32[128,2,128]{2,0,1:T(8,128)S(1)} %get-tuple-element.167, bf16[128,2,128,1]{2,1,0,3:T(2,128)(2,1)S(1)} %dynamic-slice_bitcast_fusion.2, pred[]{:T(512)S(6)} %compare.3), kind=kOutput, calls=%fused_computation.10.clone.1 | convolution fusion | flops 2151743488 | bytes 8716289 | tf_op jit(solution)/shard_map/while/body/eval_jaxpr/drxs,rsy->xdy/dot_general | solution.py:29
  179.9 8.9 %fusion.45 = f32[128,2,128]{2,0,1:T(8,128)S(1)} fusion(bf16[128,128,128]{2,1,0:T(8,128)(2,1)} %get-tuple-element.177, bf16[128,128,128]{2,0,1:T(8,128)(2,1)} %fusion.44, f32[128,2,128]{2,0,1:T(8,128)S(1)} %get-tuple-element.167, bf16[128,2,128,1]{2,1,0,3:T(2,128)(2,1)S(1)} %dynamic-slice_bitcast_fusion.2, pred[]{:T(512)S(6)} %compare.3), kind=kOutput, calls=%fused_computation.10.clone.1 | convolution fusion | flops 2151743488 | bytes 8716289 | tf_op jit(solution)/shard_map/while/body/eval_jaxpr/drxs,rsy->xdy/dot_general | solution.py:29
  196.5 8.9 %fusion.45 = f32[128,2,128]{2,0,1:T(8,128)S(1)} fusion(bf16[128,128,128]{2,1,0:T(8,128)(2,1)} %get-tuple-element.177, bf16[128,128,128]{2,0,1:T(8,128)(2,1)} %fusion.44, f32[128,2,128]{2,0,1:T(8,128)S(1)} %get-tuple-element.167, bf16[128,2,128,1]{2,1,0,3:T(2,128)(2,1)S(1)} %dynamic-slice_bitcast_fusion.2, pred[]{:T(512)S(6)} %compare.3), kind=kOutput, calls=%fused_computation.10.clone.1 | convolution fusion | flops 2151743488 | bytes 8716289 | tf_op jit(solution)/shard_map/while/body/eval_jaxpr/drxs,rsy->xdy/dot_general | solution.py:29
  213.0 8.9 %fusion.45 = f32[128,2,128]{2,0,1:T(8,128)S(1)} fusion(bf16[128,128,128]{2,1,0:T(8,128)(2,1)} %get-tuple-element.177, bf16[128,128,128]{2,0,1:T(8,128)(2,1)} %fusion.44, f32[128,2,128]{2,0,1:T(8,128)S(1)} %get-tuple-element.167, bf16[128,2,128,1]{2,1,0,3:T(2,128)(2,1)S(1)} %dynamic-slice_bitcast_fusion.2, pred[]{:T(512)S(6)} %compare.3), kind=kOutput, calls=%fused_computation.10.clone.1 | convolution fusion | flops 2151743488 | bytes 8716289 | tf_op jit(solution)/shard_map/while/body/eval_jaxpr/drxs,rsy->xdy/dot_general | solution.py:29
  229.5 8.9 %fusion.45 = f32[128,2,128]{2,0,1:T(8,128)S(1)} fusion(bf16[128,128,128]{2,1,0:T(8,128)(2,1)} %get-tuple-element.177, bf16[128,128,128]{2,0,1:T(8,128)(2,1)} %fusion.44, f32[128,2,128]{2,0,1:T(8,128)S(1)} %get-tuple-element.167, bf16[128,2,128,1]{2,1,0,3:T(2,128)(2,1)S(1)} %dynamic-slice_bitcast_fusion.2, pred[]{:T(512)S(6)} %compare.3), kind=kOutput, calls=%fused_computation.10.clone.1 | convolution fusion | flops 2151743488 | bytes 8716289 | tf_op jit(solution)/shard_map/while/body/eval_jaxpr/drxs,rsy->xdy/dot_general | solution.py:29
  246.0 8.9 %fusion.45 = f32[128,2,128]{2,0,1:T(8,128)S(1)} fusion(bf16[128,128,128]{2,1,0:T(8,128)(2,1)} %get-tuple-element.177, bf16[128,128,128]{2,0,1:T(8,128)(2,1)} %fusion.44, f32[128,2,128]{2,0,1:T(8,128)S(1)} %get-tuple-element.167, bf16[128,2,128,1]{2,1,0,3:T(2,128)(2,1)S(1)} %dynamic-slice_bitcast_fusion.2, pred[]{:T(512)S(6)} %compare.3), kind=kOutput, calls=%fused_computation.10.clone.1 | convolution fusion | flops 2151743488 | bytes 8716289 | tf_op jit(solution)/shard_map/while/body/eval_jaxpr/drxs,rsy->xdy/dot_general | solution.py:29
  262.5 8.9 %fusion.45 = f32[128,2,128]{2,0,1:T(8,128)S(1)} fusion(bf16[128,128,128]{2,1,0:T(8,128)(2,1)} %get-tuple-element.177, bf16[128,128,128]{2,0,1:T(8,128)(2,1)} %fusion.44, f32[128,2,128]{2,0,1:T(8,128)S(1)} %get-tuple-element.167, bf16[128,2,128,1]{2,1,0,3:T(2,128)(2,1)S(1)} %dynamic-slice_bitcast_fusion.2, pred[]{:T(512)S(6)} %compare.3), kind=kOutput, calls=%fused_computation.10.clone.1 | convolution fusion | flops 2151743488 | bytes 8716289 | tf_op jit(solution)/shard_map/while/body/eval_jaxpr/drxs,rsy->xdy/dot_general | solution.py:29
  279.1 8.9 %fusion.45 = f32[128,2,128]{2,0,1:T(8,128)S(1)} fusion(bf16[128,128,128]{2,1,0:T(8,128)(2,1)} %get-tuple-element.177, bf16[128,128,128]{2,0,1:T(8,128)(2,1)} %fusion.44, f32[128,2,128]{2,0,1:T(8,128)S(1)} %get-tuple-element.167, bf16[128,2,128,1]{2,1,0,3:T(2,128)(2,1)S(1)} %dynamic-slice_bitcast_fusion.2, pred[]{:T(512)S(6)} %compare.3), kind=kOutput, calls=%fused_computation.10.clone.1 | convolution fusion | flops 2151743488 | bytes 8716289 | tf_op jit(solution)/shard_map/while/body/eval_jaxpr/drxs,rsy->xdy/dot_general | solution.py:29
  295.6 8.9 %fusion.45 = f32[128,2,128]{2,0,1:T(8,128)S(1)} fusion(bf16[128,128,128]{2,1,0:T(8,128)(2,1)} %get-tuple-element.177, bf16[128,128,128]{2,0,1:T(8,128)(2,1)} %fusion.44, f32[128,2,128]{2,0,1:T(8,128)S(1)} %get-tuple-element.167, bf16[128,2,128,1]{2,1,0,3:T(2,128)(2,1)S(1)} %dynamic-slice_bitcast_fusion.2, pred[]{:T(512)S(6)} %compare.3), kind=kOutput, calls=%fused_computation.10.clone.1 | convolution fusion | flops 2151743488 | bytes 8716289 | tf_op jit(solution)/shard_map/while/body/eval_jaxpr/drxs,rsy->xdy/dot_general | solution.py:29
  312.1 8.9 %fusion.45 = f32[128,2,128]{2,0,1:T(8,128)S(1)} fusion(bf16[128,128,128]{2,1,0:T(8,128)(2,1)} %get-tuple-element.177, bf16[128,128,128]{2,0,1:T(8,128)(2,1)} %fusion.44, f32[128,2,128]{2,0,1:T(8,128)S(1)} %get-tuple-element.167, bf16[128,2,128,1]{2,1,0,3:T(2,128)(2,1)S(1)} %dynamic-slice_bitcast_fusion.2, pred[]{:T(512)S(6)} %compare.3), kind=kOutput, calls=%fused_computation.10.clone.1 | convolution fusion | flops 2151743488 | bytes 8716289 | tf_op jit(solution)/shard_map/while/body/eval_jaxpr/drxs,rsy->xdy/dot_general | solution.py:29
  328.6 8.9 %fusion.45 = f32[128,2,128]{2,0,1:T(8,128)S(1)} fusion(bf16[128,128,128]{2,1,0:T(8,128)(2,1)} %get-tuple-element.177, bf16[128,128,128]{2,0,1:T(8,128)(2,1)} %fusion.44, f32[128,2,128]{2,0,1:T(8,128)S(1)} %get-tuple-element.167, bf16[128,2,128,1]{2,1,0,3:T(2,128)(2,1)S(1)} %dynamic-slice_bitcast_fusion.2, pred[]{:T(512)S(6)} %compare.3), kind=kOutput, calls=%fused_computation.10.clone.1 | convolution fusion | flops 2151743488 | bytes 8716289 | tf_op jit(solution)/shard_map/while/body/eval_jaxpr/drxs,rsy->xdy/dot_general | solution.py:29
  339.6 49.8 %all-reduce.3.cloned.1.call-done = f32[128,2,128]{2,1,0:T(2,128)} async-done(((f32[128,2,128]{2,1,0:T(2,128)}), f32[128,2,128]{2,1,0:T(2,128)}) %all-reduce.3.cloned.1.call-update) | async-done | bytes 131088
  (43 shorter events, 106.9 us)
Async XLA Ops:
  6.5 66.6 %all-gather.2.cloned.1.call-start = ((), (), s32[]{:S(2)}) async-start(), calls=%async_computation.2 | async-start | bytes 4718592 | tf_op jit(solution)/shard_map/all_gather | solution.py:9
  42.4 29.2 %all-to-all-start = ((bf16[128,16,2,128]{3,2,1,0:T(2,128)(2,1)}), bf16[128,16,2,128]{3,2,1,0:T(2,128)(2,1)S(1)}, u32[]{:S(2)}, u32[]{:S(2)}) async-start(bf16[128,16,2,128]{3,2,1,0:T(2,128)(2,1)} %param.6), calls=%async_computation | async-start | bytes 2097152 | tf_op jit(solution)/shard_map/all_to_all | solution.py:12
  45.9 343.5 %all-reduce.3.cloned.1.call-start = ((), (), s32[]{:S(2)}) async-start(), calls=%async_computation.3 | async-start | bytes 262144
  73.2 265.2 %copy-start = (u32[32]{0:T(128)S(1)}, u32[32]{0:T(128)}, u32[]{:S(2)}) copy-start(u32[32]{0:T(128)} %constant.35) | copy-start | bytes 388
Sparse Core Ops, SparseCore 0:
  26.0 47.1 all-gather.1
  338.4 50.9 all-reduce.2
where the time goes:
time: 398 us
  matrix products  263 us (66%)
  waiting for transfers between devices  76 us (19%)
  blocking collectives  35.8 us (9%)
  between operations  14.1 us (4%)
  local copies, waits for them, and re-layouts  4.44 us (1%)
    dot_general x16, matrix products, member(): jnp.einsum('drxs,rsy->xdy', paired, iso_full, preferred_element_type=jnp....  142 us
    dot_general x16, matrix products, member(): jnp.einsum('lr,lkx->rkx', upper_slab, iso_full, preferred_element_type=jn...  121 us
    unnamed x3, waiting for transfers between devices  49.9 us
    all_to_all x1, waiting for transfers between devices, on_device(): lax.all_to_all(lower, 'bond', split_axis=0, concat_axis=1, tiled=True)  25.5 us
    all_gather x1, blocking collectives, on_device(): grouped = lax.all_gather(isometry, 'outer', axis=0, tiled=True)  19.3 us
    all_to_all x1, blocking collectives, on_device(): lax.all_to_all(upper, 'bond', split_axis=0, concat_axis=1, tiled=True)  16.5 us
  transfers between devices with their start and end apart: 3, of which 3 were waited for; matrix products, arithmetic and copies ran while one was open for 0% of the time, Pallas kernels for 0%

commit v1 on v0

v1 whole, which is shorter than its diff:
```python
import functools

import jax
import jax.numpy as jnp
from jax import lax
from jax.experimental import pallas as pl
from jax.experimental.pallas import tpu as pltpu
from jax.sharding import PartitionSpec as P

GROUP = 8
MESH = pl.DeviceIdType.MESH


def flip(index, weight):
    return index + weight * (1 - 2 * ((index // weight) % 2))


def plans(size):
    bits = [1 << b for b in range(1, size.bit_length() - 1)]
    return (bits + [1], bits[::-1] + [1])


def doubled(me, earlier):
    blocks = [me]
    for weight in earlier:
        blocks = blocks + [flip(b, weight) for b in blocks]
    return blocks


def kernel(
    bonds, outers, up_in, low, iso_in, out_ref,
    up, iso, isof, left, joined, acc, reduced,
    up_send, up_recv, iso_send, iso_recv, out_send, out_recv, red_send, red_recv,
):
    me = lax.axis_index("bond")
    my_outer = lax.axis_index("outer")
    chunks = up_in.shape[0]
    width = iso_in.shape[1]
    own = up_in.shape[2]
    per_block = iso_in.shape[0] // width
    kinds = plans(bonds)
    stages = len(kinds[0])

    barrier = pltpu.get_barrier_semaphore()
    for step in range(1, bonds):
        pl.semaphore_signal(barrier, inc=1, device_id=(lax.rem(me + step, bonds), my_outer), device_id_type=MESH)
    for step in range(1, outers):
        pl.semaphore_signal(barrier, inc=1, device_id=(me, lax.rem(my_outer + step, outers)), device_id_type=MESH)
    pl.semaphore_wait(barrier, bonds + outers - 2)

    def slot(b, o):
        return b * outers + o

    def outer_copy(step):
        return pltpu.make_async_remote_copy(
            src_ref=iso_in, dst_ref=iso.at[slot(me, my_outer)],
            send_sem=out_send.at[step], recv_sem=out_recv.at[my_outer],
            device_id=(me, lax.rem(my_outer + step, outers)), device_id_type=MESH,
        )

    def outer_arrival(step):
        source = lax.rem(my_outer + step, outers)
        return pltpu.make_async_remote_copy(
            src_ref=iso_in, dst_ref=iso.at[slot(me, source)],
            send_sem=out_send.at[step], recv_sem=out_recv.at[source],
            device_id=(me, source), device_id_type=MESH,
        )

    def up_copies(c, h, stage):
        order = kinds[h]
        partner = flip(me, order[stage])
        copies = []
        for at, block in enumerate(doubled(me, order[:stage])):
            source = up_in.at[c, h] if at == 0 else up.at[c, h, block]
            copies.append(pltpu.make_async_remote_copy(
                src_ref=source, dst_ref=up.at[c, h, block],
                send_sem=up_send.at[c, h, (1 << stage) - 1 + at], recv_sem=up_recv.at[c, h, block],
                device_id=(partner, my_outer), device_id_type=MESH,
            ))
        return copies

    def up_arrivals(c, h, stage):
        order = kinds[h]
        partner = flip(me, order[stage])
        return [
            pltpu.make_async_remote_copy(
                src_ref=up_in.at[c, h], dst_ref=up.at[c, h, block],
                send_sem=up_send.at[c, h, 0], recv_sem=up_recv.at[c, h, block],
                device_id=(partner, my_outer), device_id_type=MESH,
            )
            for block in doubled(partner, order[:stage])
        ]

    def iso_copies(o, h, stage):
        order = kinds[h]
        partner = flip(me, order[stage])
        return [
            pltpu.make_async_remote_copy(
                src_ref=iso.at[slot(block, o)], dst_ref=iso.at[slot(block, o)],
                send_sem=iso_send.at[o, (1 << stage) - 1 + at], recv_sem=iso_recv.at[o, block],
                device_id=(partner, my_outer), device_id_type=MESH,
            )
            for at, block in enumerate(doubled(me, order[:stage]))
        ]

    def iso_arrivals(o, h, stage):
        order = kinds[h]
        partner = flip(me, order[stage])
        return [
            pltpu.make_async_remote_copy(
                src_ref=iso.at[slot(block, o)], dst_ref=iso.at[slot(block, o)],
                send_sem=iso_send.at[o, 0], recv_sem=iso_recv.at[o, block],
                device_id=(partner, my_outer), device_id_type=MESH,
            )
            for block in doubled(partner, order[:stage])
        ]

    def start(copies):
        for copy in copies:
            copy.start()

    def arrive(copies):
        for copy in copies:
            copy.wait_recv()

    for step in range(1, outers):
        outer_copy(step).start()

    @pl.loop(0, chunks)
    def _(c):
        for h in range(2):
            start(up_copies(c, h, 0))

    iso[slot(me, my_outer)] = iso_in[...]

    @pl.loop(0, chunks)
    def _(c):
        for h in range(2):
            up[c, h, me] = up_in[c, h]

    for step in range(outers):
        o = lax.rem(my_outer + step, outers)
        if step:
            outer_arrival(step).wait_recv()
        start(iso_copies(o, step % 2, 0))
    for stage in range(1, stages):
        for step in range(outers):
            o = lax.rem(my_outer + step, outers)
            arrive(iso_arrivals(o, step % 2, stage - 1))
            start(iso_copies(o, step % 2, stage))

    for stage in range(1, stages - 1):
        @pl.loop(0, chunks)
        def _(c):
            for h in range(2):
                arrive(up_arrivals(c, h, stage - 1))
                start(up_copies(c, h, stage))

    def hand_over(c):
        for h in range(2):
            arrive(up_arrivals(c, h, stages - 2))
            start(up_copies(c, h, stages - 1))

    for step in range(outers):
        o = lax.rem(my_outer + step, outers)
        arrive(iso_arrivals(o, step % 2, stages - 1))

    first = pl.multiple_of(me * own, own)

    @pl.loop(0, bonds * outers)
    def _(q):
        for i in range(per_block):
            isof[pl.ds((q * per_block + i) * own, own), :] = iso[
                q, pl.ds(i * width + first, own), :
            ].astype(jnp.float32)

    @pl.loop(0, own)
    def _(k):
        left[pl.ds(k * width, width), :] = isof[pl.ds(k, width, stride=own), :].T.astype(jnp.bfloat16)

    acc[...] = jnp.zeros_like(acc)
    lowers = acc.shape[0]
    hand_over(0)

    @pl.loop(0, chunks)
    def _(c):
        @pl.when(c + 1 < chunks)
        def _():
            hand_over(c + 1)

        for h in range(2):
            arrive(up_arrivals(c, h, stages - 1))

        @pl.loop(0, 2)
        def _(h):
            for pair in range(GROUP // 2):
                w = up[c, h, :, :, pl.ds(pair * 2 * width, 2 * width)].reshape(width, 2 * width)
                j = jnp.dot(left[...], w, preferred_element_type=jnp.float32).astype(jnp.bfloat16)
                for rr in range(2):
                    for k in range(own):
                        joined[pl.ds((pair * 2 + rr) * width, width), pl.ds(k * width, width)] = j[
                            k * width:(k + 1) * width, rr * width:(rr + 1) * width
                        ]
            q = jnp.dot(joined[...], low[...], preferred_element_type=jnp.float32).astype(jnp.bfloat16)
            take = GROUP // per_block
            rows = iso[pl.ds((c * 2 + h) * take, take)].reshape(GROUP * width, width)
            for d in range(lowers):
                lhs = jnp.concatenate(
                    [q[rr * width:(rr + 1) * width, d * width:(d + 1) * width] for rr in range(GROUP)], axis=1
                )
                acc[d] += jnp.dot(lhs, rows, preferred_element_type=jnp.float32).reshape(acc.shape[1:])

    def red_copy(step):
        target = lax.rem(me + step, bonds)
        return pltpu.make_async_remote_copy(
            src_ref=acc.at[:, target], dst_ref=reduced.at[step - 1],
            send_sem=red_send.at[step], recv_sem=red_recv.at[step],
            device_id=(target, my_outer), device_id_type=MESH,
        )

    for step in range(1, bonds):
        red_copy(step).start()
    total = acc[:, me]
    for step in range(1, bonds):
        red_copy(step).wait_recv()
        total = total + reduced[step - 1]
    out_ref[...] = total
    for step in range(1, bonds):
        red_copy(step).wait_send()
    for step in range(1, outers):
        outer_copy(step).wait_send()
    for stage in range(stages):
        for step in range(outers):
            o = lax.rem(my_outer + step, outers)
            for copy in iso_copies(o, step % 2, stage):
                copy.wait_send()

    @pl.loop(0, chunks)
    def _(c):
        for h in range(2):
            for stage in range(stages):
                for copy in up_copies(c, h, stage):
                    copy.wait_send()


def fused(upper, lower, isometry):
    bonds, outers = lax.axis_size("bond"), lax.axis_size("outer")
    width = isometry.shape[1]
    own, lowers = upper.shape[1], lower.shape[2]
    chunks = width // (2 * GROUP)
    up_in = upper.transpose(1, 2, 0).reshape(own, chunks, 2, GROUP * width).transpose(1, 2, 0, 3)
    low = lower.transpose(1, 0, 2, 3).reshape(own * width, lowers * width)
    bf, f32, dma = jnp.bfloat16, jnp.float32, pltpu.SemaphoreType.DMA
    out = pl.pallas_call(
        functools.partial(kernel, bonds, outers),
        out_shape=jax.ShapeDtypeStruct((lowers, own, width), f32),
        in_specs=[pl.BlockSpec(memory_space=pltpu.VMEM)] * 3,
        out_specs=pl.BlockSpec(memory_space=pltpu.VMEM),
        scratch_shapes=[
            pltpu.VMEM((chunks, 2, bonds, own, GROUP * width), bf),
            pltpu.VMEM((bonds * outers, isometry.shape[0], width), bf),
            pltpu.VMEM((width * own, width), f32),
            pltpu.VMEM((own * width, width), bf),
            pltpu.VMEM((GROUP * width, own * width), bf),
            pltpu.VMEM((lowers, bonds, own, width), f32),
            pltpu.VMEM((bonds - 1, lowers, own, width), f32),
            dma((chunks, 2, bonds - 1)),
            dma((chunks, 2, bonds)),
            dma((outers, bonds - 1)),
            dma((outers, bonds)),
            dma((outers,)),
            dma((outers,)),
            dma((bonds,)),
            dma((bonds,)),
        ],
        compiler_params=pltpu.CompilerParams(
            collective_id=0, has_side_effects=True, vmem_limit_bytes=60 * 1024 * 1024
        ),
    )(up_in, low, isometry)
    return out.transpose(1, 0, 2)


def plain(upper, lower, isometry):
    width = isometry.shape[1]
    own = upper.shape[1]
    iso = lax.all_gather(isometry, ("bond", "outer"), axis=0, tiled=True).reshape(width, width, width)
    whole = lax.all_gather(upper, "bond", axis=1, tiled=True)
    mine = lax.dynamic_slice_in_dim(iso, lax.axis_index("bond") * own, own, 1)

    def column(total, item):
        slab, rows = item
        joined = jnp.einsum("ml,lkx->xkm", slab, mine, preferred_element_type=jnp.float32).astype(jnp.bfloat16)
        paired = jnp.einsum("xkm,mkds->xds", joined, lower, preferred_element_type=jnp.float32).astype(jnp.bfloat16)
        return total + jnp.einsum("xds,sy->xdy", paired, rows, preferred_element_type=jnp.float32), None

    start_total = jnp.zeros((width, lower.shape[2], width), jnp.float32)
    total, _ = lax.scan(column, start_total, (whole.transpose(2, 0, 1), iso))
    return lax.psum_scatter(total, "bond", scatter_dimension=0, tiled=True)


def on_device(upper, lower, isometry):
    bonds = lax.axis_size("bond")
    width = isometry.shape[1]
    rows = isometry.shape[0] // width
    fits = (
        upper.shape[1] % 16 == 0 and bonds >= 4 and bonds & (bonds - 1) == 0
        and width % (2 * GROUP) == 0 and rows > 0 and GROUP % rows == 0
    )
    return (fused if fits else plain)(upper, lower, isometry)


def solution(mesh):
    return jax.shard_map(
        on_device,
        mesh=mesh,
        in_specs=(
            P(None, "bond", None),
            P(None, "bond", "outer", None),
            P(("bond", "outer"), None),
        ),
        out_specs=P("bond", "outer", None),
        check_vma=False,
    )
```

time: 398 us -> 123 us (0.31)
  matrix products: 263 us -> 0 us
  Pallas kernels: 0 us -> 114 us
  waiting for transfers between devices: 76 us -> 0 us
  blocking collectives: 35.8 us -> 0 us
  between operations: 14.1 us -> 0.03 us
    dot_general x32 -> x0, matrix products: 263 us -> none  [the longest x16 142 us: member(): jnp.einsum('drxs,rsy->xdy', paired, iso_full, preferred_element_type=jnp....]
    pallas_call x0 -> x1, Pallas kernels: none -> 114 us  [fused(): pl.pallas_call(functools.partial(kernel, bonds, outers), out_shape=jax.Sh...]
    unnamed x3 -> x0, waiting for transfers between devices: 49.9 us -> none
    all_to_all x1 -> x0, waiting for transfers between devices: 25.5 us -> none  [on_device(): lax.all_to_all(lower, 'bond', split_axis=0, concat_axis=1, tiled=True)]
    all_gather x1 -> x0, blocking collectives: 19.3 us -> none  [on_device(): grouped = lax.all_gather(isometry, 'outer', axis=0, tiled=True)]
    all_to_all x1 -> x0, blocking collectives: 16.5 us -> none  [on_device(): lax.all_to_all(upper, 'bond', split_axis=0, concat_axis=1, tiled=True)]
  transfers between devices with their start and end apart: 3 -> 0, of which waited for: 3 -> 0; matrix products, arithmetic and copies ran while one was open for 0% -> 0% of each run, Pallas kernels for 0% -> 0%
where the time goes in v1:
time: 123 us; the launch traced here: 120 us
  Pallas kernels  114 us (93%)
  local copies, waits for them, and re-layouts  6.34 us (5%)
    pallas_call x1, Pallas kernels, fused(): pl.pallas_call(functools.partial(kernel, bonds, outers), out_shape=jax.Sh...  114 us

profile of v1, /device:TPU:0, one launch (start us, length us, event | category | flops | bytes accessed | tf_op | source)
XLA Modules:
  0.0 120.4 jit_solution(7417016167251112308)
XLA Ops:
  0.0 2.2 %copy.8 = bf16[16,128,2,128]{3,2,1,0:T(2,128)(2,1)S(1)} copy(bf16[16,128,2,128]{3,2,0,1:T(2,128)(2,1)} %bitcast.14) | data formatting | bytes 2097152 | tf_op jit(solution)/shard_map/transpose | solution.py:252
  2.2 0.0 copy-start
  2.2 1.1 copy.13
  3.3 0.0 copy-done
  3.3 0.5 copy.6
  3.8 0.1 reshape.6
  3.9 1.1 copy.14
  5.0 114.0 %shard_map.37 = f32[2,16,128]{2,1,0:T(8,128)} custom-call(bf16[8,2,16,1024]{3,2,1,0:T(8,128)(2,1)} %bitcast.13, bf16[2048,256]{1,0:T(8,128)(2,1)} %bitcast.11, bf16[512,128]{1,0:T(8,128)(2,1)} %iso_in.1), custom_call_target="tpu_custom_call" | custom-call | tf_op jit(solution)/shard_map/pallas_call | solution.py:254
  119.1 1.3 %copy.9 = f32[16,2,128]{2,1,0:T(2,128)} copy(f32[16,2,128]{2,0,1:T(8,128)} %bitcast.16) | data formatting | bytes 32768 | tf_op jit(solution)/shard_map/transpose | solution.py:280
Async XLA Ops:
  2.2 1.1 copy-start

commit v2 on v1

--- a/solution.py
+++ b/solution.py
@@ -29,27 +29,46 @@
 
 def kernel(
     bonds, outers, up_in, low, iso_in, out_ref,
-    up, iso, isof, left, joined, acc, reduced,
-    up_send, up_recv, iso_send, iso_recv, out_send, out_recv, red_send, red_recv,
+    up, iso, thin, isof, left, joined, pairs, acc, reduced,
+    thin_send, thin_recv, up_send, up_recv, iso_send, iso_recv, out_send, out_recv, red_send, red_recv,
 ):
     me = lax.axis_index("bond")
     my_outer = lax.axis_index("outer")
-    chunks = up_in.shape[0]
-    width = iso_in.shape[1]
+    chunks = up_in.shape[0] // 2
+    per_block, width = iso_in.shape[:2]
     own = up_in.shape[2]
-    per_block = iso_in.shape[0] // width
+    lowers = low.shape[0]
     kinds = plans(bonds)
     stages = len(kinds[0])
 
     barrier = pltpu.get_barrier_semaphore()
-    for step in range(1, bonds):
-        pl.semaphore_signal(barrier, inc=1, device_id=(lax.rem(me + step, bonds), my_outer), device_id_type=MESH)
-    for step in range(1, outers):
-        pl.semaphore_signal(barrier, inc=1, device_id=(me, lax.rem(my_outer + step, outers)), device_id_type=MESH)
-    pl.semaphore_wait(barrier, bonds + outers - 2)
+    peers = [
+        (lax.rem(me + i, bonds), lax.rem(my_outer + j, outers))
+        for i in range(bonds) for j in range(outers) if i or j
+    ]
+    for peer in peers:
+        pl.semaphore_signal(barrier, inc=1, device_id=peer, device_id_type=MESH)
+    pl.semaphore_wait(barrier, len(peers))
 
     def slot(b, o):
         return b * outers + o
+
+    def thin_copy(at):
+        b, o = peers[at]
+        return pltpu.make_async_remote_copy(
+            src_ref=iso_in.at[:, pl.ds(pl.multiple_of(b * own, own), own)],
+            dst_ref=thin.at[slot(me, my_outer)],
+            send_sem=thin_send.at[at], recv_sem=thin_recv.at[slot(me, my_outer)],
+            device_id=(b, o), device_id_type=MESH,
+        )
+
+    def thin_arrival(at):
+        b, o = peers[at]
+        return pltpu.make_async_remote_copy(
+            src_ref=thin.at[slot(b, o)], dst_ref=thin.at[slot(b, o)],
+            send_sem=thin_send.at[at], recv_sem=thin_recv.at[slot(b, o)],
+            device_id=(b, o), device_id_type=MESH,
+        )
 
     def outer_copy(step):
         return pltpu.make_async_remote_copy(
@@ -71,9 +90,9 @@
         partner = flip(me, order[stage])
         copies = []
         for at, block in enumerate(doubled(me, order[:stage])):
-            source = up_in.at[c, h] if at == 0 else up.at[c, h, block]
+            source = up_in.at[c * 2 + h] if at == 0 else up.at[c * 2 + h, block]
             copies.append(pltpu.make_async_remote_copy(
-                src_ref=source, dst_ref=up.at[c, h, block],
+                src_ref=source, dst_ref=up.at[c * 2 + h, block],
                 send_sem=up_send.at[c, h, (1 << stage) - 1 + at], recv_sem=up_recv.at[c, h, block],
                 device_id=(partner, my_outer), device_id_type=MESH,
             ))
@@ -84,7 +103,7 @@
         partner = flip(me, order[stage])
         return [
             pltpu.make_async_remote_copy(
-                src_ref=up_in.at[c, h], dst_ref=up.at[c, h, block],
+                src_ref=up_in.at[c * 2 + h], dst_ref=up.at[c * 2 + h, block],
                 send_sem=up_send.at[c, h, 0], recv_sem=up_recv.at[c, h, block],
                 device_id=(partner, my_outer), device_id_type=MESH,
             )
@@ -123,6 +142,8 @@
         for copy in copies:
             copy.wait_recv()
 
+    for at in range(len(peers)):
+        thin_copy(at).start()
     for step in range(1, outers):
         outer_copy(step).start()
 
@@ -131,23 +152,15 @@
         for h in range(2):
             start(up_copies(c, h, 0))
 
+    first = pl.multiple_of(me * own, own)
     iso[slot(me, my_outer)] = iso_in[...]
-
-    @pl.loop(0, chunks)
-    def _(c):
-        for h in range(2):
-            up[c, h, me] = up_in[c, h]
-
-    for step in range(outers):
-        o = lax.rem(my_outer + step, outers)
-        if step:
-            outer_arrival(step).wait_recv()
-        start(iso_copies(o, step % 2, 0))
-    for stage in range(1, stages):
-        for step in range(outers):
-            o = lax.rem(my_outer + step, outers)
-            arrive(iso_arrivals(o, step % 2, stage - 1))
-            start(iso_copies(o, step % 2, stage))
+    thin[slot(me, my_outer)] = iso_in[:, pl.ds(first, own)]
+
+    @pl.loop(0, 2 * chunks)
+    def _(g):
+        up[g, me] = up_in[g]
+
+    acc[...] = jnp.zeros_like(acc)
 
     for stage in range(1, stages - 1):
         @pl.loop(0, chunks)
@@ -161,26 +174,30 @@
             arrive(up_arrivals(c, h, stages - 2))
             start(up_copies(c, h, stages - 1))
 
-    for step in range(outers):
-        o = lax.rem(my_outer + step, outers)
-        arrive(iso_arrivals(o, step % 2, stages - 1))
-
-    first = pl.multiple_of(me * own, own)
+    def iso_stage(stage):
+        for step in range(outers):
+            o = lax.rem(my_outer + step, outers)
+            if stage:
+                arrive(iso_arrivals(o, step % 2, stage - 1))
+            elif step:
+                outer_arrival(step).wait_recv()
+            if stage < stages:
+                start(iso_copies(o, step % 2, stage))
+
+    for at in range(len(peers)):
+        thin_arrival(at).wait_recv()
+    hand_over(0)
 
     @pl.loop(0, bonds * outers)
     def _(q):
         for i in range(per_block):
-            isof[pl.ds((q * per_block + i) * own, own), :] = iso[
-                q, pl.ds(i * width + first, own), :
-            ].astype(jnp.float32)
+            isof[pl.ds((q * per_block + i) * own, own), :] = thin[q, i].astype(jnp.float32)
 
     @pl.loop(0, own)
     def _(k):
         left[pl.ds(k * width, width), :] = isof[pl.ds(k, width, stride=own), :].T.astype(jnp.bfloat16)
 
-    acc[...] = jnp.zeros_like(acc)
-    lowers = acc.shape[0]
-    hand_over(0)
+    pace = max(1, (chunks - 1) // stages)
 
     @pl.loop(0, chunks)
     def _(c):
@@ -188,27 +205,42 @@
         def _():
             hand_over(c + 1)
 
+        for stage in range(stages):
+            @pl.when(c == min(chunks - 1, 1 + stage * pace))
+            def _():
+                iso_stage(stage)
+
         for h in range(2):
             arrive(up_arrivals(c, h, stages - 1))
 
         @pl.loop(0, 2)
         def _(h):
+            g = c * 2 + h
             for pair in range(GROUP // 2):
-                w = up[c, h, :, :, pl.ds(pair * 2 * width, 2 * width)].reshape(width, 2 * width)
+                w = jnp.concatenate(
+                    [up[g, :, 2 * pair + rr].reshape(width, width) for rr in range(2)], axis=1
+                )
                 j = jnp.dot(left[...], w, preferred_element_type=jnp.float32).astype(jnp.bfloat16)
                 for rr in range(2):
                     for k in range(own):
                         joined[pl.ds((pair * 2 + rr) * width, width), pl.ds(k * width, width)] = j[
                             k * width:(k + 1) * width, rr * width:(rr + 1) * width
                         ]
-            q = jnp.dot(joined[...], low[...], preferred_element_type=jnp.float32).astype(jnp.bfloat16)
-            take = GROUP // per_block
-            rows = iso[pl.ds((c * 2 + h) * take, take)].reshape(GROUP * width, width)
-            for d in range(lowers):
-                lhs = jnp.concatenate(
-                    [q[rr * width:(rr + 1) * width, d * width:(d + 1) * width] for rr in range(GROUP)], axis=1
-                )
-                acc[d] += jnp.dot(lhs, rows, preferred_element_type=jnp.float32).reshape(acc.shape[1:])
+            right = jnp.concatenate([low[d] for d in range(lowers)], axis=1)
+            pairs[g] = jnp.dot(joined[...], right, preferred_element_type=jnp.float32).astype(jnp.bfloat16)
+
+    iso_stage(stages)
+    take = GROUP // per_block
+
+    @pl.loop(0, 2 * chunks)
+    def _(g):
+        rows = iso[pl.ds(g * take, take)].reshape(GROUP * width, width)
+        lhs = jnp.concatenate([
+            jnp.concatenate([
+                pairs[g, pl.ds(rr * width, width), pl.ds(d * width, width)] for rr in range(GROUP)
+            ], axis=1) for d in range(lowers)
+        ], axis=0)
+        acc[...] += jnp.dot(lhs, rows, preferred_element_type=jnp.float32).reshape(acc.shape)
 
     def red_copy(step):
         target = lax.rem(me + step, bonds)
@@ -227,6 +259,8 @@
     out_ref[...] = total
     for step in range(1, bonds):
         red_copy(step).wait_send()
+    for at in range(len(peers)):
+        thin_copy(at).wait_send()
     for step in range(1, outers):
         outer_copy(step).wait_send()
     for stage in range(stages):
@@ -247,9 +281,10 @@
     bonds, outers = lax.axis_size("bond"), lax.axis_size("outer")
     width = isometry.shape[1]
     own, lowers = upper.shape[1], lower.shape[2]
-    chunks = width // (2 * GROUP)
-    up_in = upper.transpose(1, 2, 0).reshape(own, chunks, 2, GROUP * width).transpose(1, 2, 0, 3)
-    low = lower.transpose(1, 0, 2, 3).reshape(own * width, lowers * width)
+    groups = width // GROUP
+    up_in = upper.transpose(2, 1, 0).reshape(groups, GROUP, own, width)
+    low = lower.transpose(2, 1, 0, 3).reshape(lowers, own * width, width)
+    iso_in = isometry.reshape(-1, width, width)
     bf, f32, dma = jnp.bfloat16, jnp.float32, pltpu.SemaphoreType.DMA
     out = pl.pallas_call(
         functools.partial(kernel, bonds, outers),
@@ -257,15 +292,19 @@
         in_specs=[pl.BlockSpec(memory_space=pltpu.VMEM)] * 3,
         out_specs=pl.BlockSpec(memory_space=pltpu.VMEM),
         scratch_shapes=[
-            pltpu.VMEM((chunks, 2, bonds, own, GROUP * width), bf),
-            pltpu.VMEM((bonds * outers, isometry.shape[0], width), bf),
+            pltpu.VMEM((groups, bonds, GROUP, own, width), bf),
+            pltpu.VMEM((bonds * outers, *iso_in.shape), bf),
+            pltpu.VMEM((bonds * outers, iso_in.shape[0], own, width), bf),
             pltpu.VMEM((width * own, width), f32),
             pltpu.VMEM((own * width, width), bf),
             pltpu.VMEM((GROUP * width, own * width), bf),
+            pltpu.VMEM((groups, GROUP * width, lowers * width), bf),
             pltpu.VMEM((lowers, bonds, own, width), f32),
             pltpu.VMEM((bonds - 1, lowers, own, width), f32),
-            dma((chunks, 2, bonds - 1)),
-            dma((chunks, 2, bonds)),
+            dma((bonds * outers - 1,)),
+            dma((bonds * outers,)),
+            dma((groups // 2, 2, bonds - 1)),
+            dma((groups // 2, 2, bonds)),
             dma((outers, bonds - 1)),
             dma((outers, bonds)),
             dma((outers,)),
@@ -276,7 +315,7 @@
         compiler_params=pltpu.CompilerParams(
             collective_id=0, has_side_effects=True, vmem_limit_bytes=60 * 1024 * 1024
         ),
-    )(up_in, low, isometry)
+    )(up_in, low, iso_in)
     return out.transpose(1, 0, 2)
 
 

time: 123 us -> 111 us (0.902); the launches traced: 120 us -> 111 us
  Pallas kernels: 114 us -> 105 us
    pallas_call x1, Pallas kernels: 114 us -> 105 us  [fused(): pl.pallas_call(functools.partial(kernel, bonds, outers), out_shape=jax.Sh...]
    transpose x2, local copies, waits for them, and re-layouts: 2.65 us -> 3.99 us  [the longest x1 2.59 us: fused(): up_in = upper.transpose(2, 1, 0).reshape(groups, GROUP, own, width)]
    reshape x2 -> x0, local copies, waits for them, and re-layouts: 1.23 us -> none  [fused(): upper.transpose(1, 2, 0).reshape(own, chunks, 2, GROUP * width)]
where the time goes in v2:
time: 111 us
  Pallas kernels  105 us (95%)
  local copies, waits for them, and re-layouts  5.32 us (5%)
    pallas_call x1, Pallas kernels, fused(): pl.pallas_call(functools.partial(kernel, bonds, outers), out_shape=jax.Sh...  105 us
    transpose x1, local copies, waits for them, and re-layouts, fused(): up_in = upper.transpose(2, 1, 0).reshape(groups, GROUP, own, width)  2.59 us

profile of v2, /device:TPU:0, one launch (start us, length us, event | category | flops | bytes accessed | tf_op | source)
XLA Modules:
  0.0 110.8 jit_solution(10071447626880781450)
XLA Ops:
  0.0 0.0 copy-start
  0.0 2.6 %copy.4 = bf16[128,16,128]{2,1,0:T(8,128)(2,1)} copy(bf16[128,16,128]{0,1,2:T(8,128)(2,1)} %bitcast.9) | data formatting | bytes 1048576 | tf_op jit(solution)/shard_map/transpose | solution.py:285
  2.6 0.0 copy-done
  2.6 1.4 %copy.5 = bf16[2,16,128,128]{3,2,1,0:T(8,128)(2,1)} copy(bf16[2,16,128,128]{3,0,1,2:T(2,128)(2,1)S(1)} %bitcast.8) | data formatting | bytes 2097152 | tf_op jit(solution)/shard_map/transpose | solution.py:286
  4.0 105.5 %shard_map.37 = f32[2,16,128]{2,1,0:T(8,128)} custom-call(bf16[16,8,16,128]{3,2,1,0:T(8,128)(2,1)} %bitcast.7, bf16[2,2048,128]{2,1,0:T(8,128)(2,1)} %bitcast.6, bf16[4,128,128]{2,1,0:T(8,128)(2,1)} %bitcast.10), custom_call_target="tpu_custom_call" | custom-call | tf_op jit(solution)/shard_map/pallas_call | solution.py:289
  109.5 1.3 %copy.6 = f32[16,2,128]{2,1,0:T(2,128)} copy(f32[16,2,128]{2,0,1:T(8,128)} %bitcast.11) | data formatting | bytes 32768 | tf_op jit(solution)/shard_map/transpose | solution.py:319
Async XLA Ops:
  0.0 2.6 %copy-start = (bf16[128,16,2,128]{3,2,1,0:T(2,128)(2,1)S(1)}, bf16[128,16,2,128]{3,2,1,0:T(2,128)(2,1)}, u32[]{:S(2)}) copy-start(bf16[128,16,2,128]{3,2,1,0:T(2,128)(2,1)} %param.4) | copy-start | bytes 3145732

commit v3 on v2

--- a/solution.py
+++ b/solution.py
@@ -213,21 +213,20 @@
         for h in range(2):
             arrive(up_arrivals(c, h, stages - 1))
 
+        for pair in range(GROUP):
+            h, at = divmod(2 * pair, GROUP)
+            w = jnp.concatenate([up[c * 2 + h, :, at + rr].reshape(width, width) for rr in range(2)], axis=1)
+            j = jnp.dot(left[...], w, preferred_element_type=jnp.float32).astype(jnp.bfloat16)
+            for rr in range(2):
+                for k in range(own):
+                    joined[h, pl.ds((at + rr) * width, width), pl.ds(k * width, width)] = j[
+                        k * width:(k + 1) * width, rr * width:(rr + 1) * width
+                    ]
+        right = jnp.concatenate([low[d] for d in range(lowers)], axis=1)
+
         @pl.loop(0, 2)
         def _(h):
-            g = c * 2 + h
-            for pair in range(GROUP // 2):
-                w = jnp.concatenate(
-                    [up[g, :, 2 * pair + rr].reshape(width, width) for rr in range(2)], axis=1
-                )
-                j = jnp.dot(left[...], w, preferred_element_type=jnp.float32).astype(jnp.bfloat16)
-                for rr in range(2):
-                    for k in range(own):
-                        joined[pl.ds((pair * 2 + rr) * width, width), pl.ds(k * width, width)] = j[
-                            k * width:(k + 1) * width, rr * width:(rr + 1) * width
-                        ]
-            right = jnp.concatenate([low[d] for d in range(lowers)], axis=1)
-            pairs[g] = jnp.dot(joined[...], right, preferred_element_type=jnp.float32).astype(jnp.bfloat16)
+            pairs[c * 2 + h] = jnp.dot(joined[h], right, preferred_element_type=jnp.float32).astype(jnp.bfloat16)
 
     iso_stage(stages)
     take = GROUP // per_block
@@ -297,7 +296,7 @@
             pltpu.VMEM((bonds * outers, iso_in.shape[0], own, width), bf),
             pltpu.VMEM((width * own, width), f32),
             pltpu.VMEM((own * width, width), bf),
-            pltpu.VMEM((GROUP * width, own * width), bf),
+            pltpu.VMEM((2, GROUP * width, own * width), bf),
             pltpu.VMEM((groups, GROUP * width, lowers * width), bf),
             pltpu.VMEM((lowers, bonds, own, width), f32),
             pltpu.VMEM((bonds - 1, lowers, own, width), f32),

time: 111 us -> 92.3 us (0.83)
  Pallas kernels: 105 us -> 86.8 us
    pallas_call x1, Pallas kernels: 105 us -> 86.8 us  [fused(): pl.pallas_call(functools.partial(kernel, bonds, outers), out_shape=jax.Sh...]
where the time goes in v3:
time: 92.3 us; the launch traced here: 92.1 us
  Pallas kernels  86.8 us (94%)
  local copies, waits for them, and re-layouts  5.32 us (6%)
    pallas_call x1, Pallas kernels, fused(): pl.pallas_call(functools.partial(kernel, bonds, outers), out_shape=jax.Sh...  86.8 us
    transpose x1, local copies, waits for them, and re-layouts, fused(): up_in = upper.transpose(2, 1, 0).reshape(groups, GROUP, own, width)  2.59 us

profile of v3, /device:TPU:0, one launch (start us, length us, event | category | flops | bytes accessed | tf_op | source)
XLA Modules:
  0.0 92.1 jit_solution(1842884817603131387)
XLA Ops:
  0.0 0.0 copy-start
  0.0 2.6 %copy.4 = bf16[128,16,128]{2,1,0:T(8,128)(2,1)} copy(bf16[128,16,128]{0,1,2:T(8,128)(2,1)} %bitcast.9) | data formatting | bytes 1048576 | tf_op jit(solution)/shard_map/transpose | solution.py:284
  2.6 0.0 copy-done
  2.6 1.4 %copy.5 = bf16[2,16,128,128]{3,2,1,0:T(8,128)(2,1)} copy(bf16[2,16,128,128]{3,0,1,2:T(2,128)(2,1)S(1)} %bitcast.8) | data formatting | bytes 2097152 | tf_op jit(solution)/shard_map/transpose | solution.py:285
  4.0 86.8 %shard_map.37 = f32[2,16,128]{2,1,0:T(8,128)} custom-call(bf16[16,8,16,128]{3,2,1,0:T(8,128)(2,1)} %bitcast.7, bf16[2,2048,128]{2,1,0:T(8,128)(2,1)} %bitcast.6, bf16[4,128,128]{2,1,0:T(8,128)(2,1)} %bitcast.10), custom_call_target="tpu_custom_call" | custom-call | tf_op jit(solution)/shard_map/pallas_call | solution.py:288
  90.8 1.3 %copy.6 = f32[16,2,128]{2,1,0:T(2,128)} copy(f32[16,2,128]{2,0,1:T(8,128)} %bitcast.11) | data formatting | bytes 32768 | tf_op jit(solution)/shard_map/transpose | solution.py:318
Async XLA Ops:
  0.0 2.6 %copy-start = (bf16[128,16,2,128]{3,2,1,0:T(2,128)(2,1)S(1)}, bf16[128,16,2,128]{3,2,1,0:T(2,128)(2,1)}, u32[]{:S(2)}) copy-start(bf16[128,16,2,128]{3,2,1,0:T(2,128)(2,1)} %param.4) | copy-start | bytes 3145732

commit v4 on v3

--- a/solution.py
+++ b/solution.py
@@ -224,9 +224,11 @@
                     ]
         right = jnp.concatenate([low[d] for d in range(lowers)], axis=1)
 
-        @pl.loop(0, 2)
-        def _(h):
-            pairs[c * 2 + h] = jnp.dot(joined[h], right, preferred_element_type=jnp.float32).astype(jnp.bfloat16)
+        @pl.when(c >= 0)
+        def _():
+            flat = joined[...].reshape(2 * GROUP * width, own * width)
+            product = jnp.dot(flat, right, preferred_element_type=jnp.float32).astype(jnp.bfloat16)
+            pairs[pl.ds(c * 2, 2)] = product.reshape(2, *pairs.shape[1:])
 
     iso_stage(stages)
     take = GROUP // per_block

time: 92.3 us -> 91.4 us (level)
  no operation moved by 1% of the time
where the time goes in v4:
time: 91.4 us; the launch traced here: 91.2 us
  Pallas kernels  85.9 us (94%)
  local copies, waits for them, and re-layouts  5.32 us (6%)
    pallas_call x1, Pallas kernels, fused(): pl.pallas_call(functools.partial(kernel, bonds, outers), out_shape=jax.Sh...  85.9 us
    transpose x1, local copies, waits for them, and re-layouts, fused(): up_in = upper.transpose(2, 1, 0).reshape(groups, GROUP, own, width)  2.59 us

profile of v4, /device:TPU:0, one launch (start us, length us, event | category | flops | bytes accessed | tf_op | source)
XLA Modules:
  0.0 91.2 jit_solution(15408323599829158487)
XLA Ops:
  0.0 0.0 copy-start
  0.0 2.6 %copy.4 = bf16[128,16,128]{2,1,0:T(8,128)(2,1)} copy(bf16[128,16,128]{0,1,2:T(8,128)(2,1)} %bitcast.9) | data formatting | bytes 1048576 | tf_op jit(solution)/shard_map/transpose | solution.py:286
  2.6 0.0 copy-done
  2.6 1.4 %copy.5 = bf16[2,16,128,128]{3,2,1,0:T(8,128)(2,1)} copy(bf16[2,16,128,128]{3,0,1,2:T(2,128)(2,1)S(1)} %bitcast.8) | data formatting | bytes 2097152 | tf_op jit(solution)/shard_map/transpose | solution.py:287
  4.0 85.9 %shard_map.37 = f32[2,16,128]{2,1,0:T(8,128)} custom-call(bf16[16,8,16,128]{3,2,1,0:T(8,128)(2,1)} %bitcast.7, bf16[2,2048,128]{2,1,0:T(8,128)(2,1)} %bitcast.6, bf16[4,128,128]{2,1,0:T(8,128)(2,1)} %bitcast.10), custom_call_target="tpu_custom_call" | custom-call | tf_op jit(solution)/shard_map/pallas_call | solution.py:290
  89.9 1.3 %copy.6 = f32[16,2,128]{2,1,0:T(2,128)} copy(f32[16,2,128]{2,0,1:T(8,128)} %bitcast.11) | data formatting | bytes 32768 | tf_op jit(solution)/shard_map/transpose | solution.py:320
Async XLA Ops:
  0.0 2.6 %copy-start = (bf16[128,16,2,128]{3,2,1,0:T(2,128)(2,1)S(1)}, bf16[128,16,2,128]{3,2,1,0:T(2,128)(2,1)}, u32[]{:S(2)}) copy-start(bf16[128,16,2,128]{3,2,1,0:T(2,128)(2,1)} %param.4) | copy-start | bytes 3145732
